TPU v7x, 128 devices: a whole 4x4x4 slice. The times are simulated.
128 devices in a mesh: row: 8 (over z, core), col: 16 (over y, x).
Axes of the slice: x: 4, y: 4, z: 4, core: 2. Of those that a mesh axis runs over, the one named last changes fastest.
Arguments:
- panel_first: bfloat16 [128, 256, 1024], P(('row', 'col')), may hold values from -3 to 3
- panel_second: bfloat16 [128, 256, 1024], P(('row', 'col')), may hold values from -4 to 4
- diag_first: bfloat16 [1024, 1024], P('col'), as said below
- bridge: bfloat16 [1024, 1024], P('col'), may hold values from -0.024902344 to 0.024902344
- diag_second: bfloat16 [1024, 1024], P('col'), as said below
- trailing: float32 [128, 24, 256, 256], P(('row', 'col')), may hold values from -6 to 6
- trail_pairs: int32 [128, 2, 24], P(('row', 'col')), may hold values from 0 to 15, as said below
- live_count: int32 [128], P(('row', 'col')), may hold values from 1 to 24, as said below
Outputs:
- lower_first: bfloat16 [128, 256, 1024], P(('row', 'col'))
- lower_second: bfloat16 [128, 256, 1024], P(('row', 'col'))
- trailing_out: float32 [128, 24, 256, 256], P(('row', 'col'))
Inputs may be any that keep to these rules, and one draw needn't show every extreme that they name: `trail_pairs`: on each device the listed pairs are distinct; the first entry of a pair is below 16 and the second below 8. `live_count`: some device has all 24 slots live in every draw. `diag_first`: symmetric and positive definite, with diagonal entries between 0.75 and 2.3. `diag_second`: symmetric and positive definite, with diagonal entries between 3.4 and 7.5.
All inputs are finite; a program needn't handle non-finite values.
Results may differ from a plain program's by a relative error of at most 0.001.
Values may be sent and summed in bfloat16 or wider, within the bound.
No kernel may reach another device: no remote copies, remote signals or barrier semaphores. Data moves between devices by JAX's collectives and lax.ppermute only.
A program may use at most 192 MiB of HBM per device.

v0:
```python
import functools

import jax
import jax.numpy as jnp
from jax import lax
from jax.experimental import pallas as pl
from jax.experimental.pallas import tpu as pltpu
from jax.sharding import PartitionSpec as P

F32, BF16 = jnp.float32, jnp.bfloat16
N, NB, Q = 1024, 128, 8


def split(x):
    hi = x.astype(BF16)
    return hi, (x - hi.astype(F32)).astype(BF16)


def dot(a, b, dims):
    return lax.dot_general(a, b, (dims, ((), ())), preferred_element_type=F32)


def diag_inverse(tiles, far_from=None):
    count = len(tiles)
    shape = (Q, NB)
    sub = lax.broadcasted_iota(jnp.int32, shape, 0)
    lane = lax.broadcasted_iota(jnp.int32, shape, 1)
    wide = lambda v: jnp.broadcast_to(v, shape)
    lanes = lambda v, c: jnp.take_along_axis(v, jnp.full(shape, c, jnp.int32), axis=1)
    zero = jnp.zeros(shape, F32)
    tiles = list(tiles)
    out = []

    def total(terms):
        while len(terms) > 1:
            terms = [a + b for a, b in zip(terms[::2], terms[1::2])] + ([terms[-1]] if len(terms) % 2 else [])
        return terms[0]

    def small(e):
        r, l, v = [], {}, {}
        for m in range(Q):
            rm = lax.rsqrt(e[m, m])
            r.append(rm)
            for i in range(m + 1, Q):
                l[i, m] = e[i, m] * rm
            for j in range(m + 1, Q):
                for i in range(j, Q):
                    e[i, j] = e[i, j] - l[i, m] * l[j, m]
            v[m, m] = rm
            for k in range(m):
                v[m, k] = -(rm * total([l[m, j] * v[j, k] for j in range(k, m)]))
        return v

    def assemble(coef):
        cols = []
        for k in range(Q):
            col = zero
            for i in range(Q):
                got = coef(i, k)
                if got is not None:
                    col = jnp.where(sub == i, got, col)
            cols.append(col)
        return cols

    def spread_rows(x):
        return [wide(x[k : k + 1, :]) for k in range(Q)]

    def apply(cols, rows):
        return total([c * x for c, x in zip(cols, rows)])

    for s in range(0, count, 2):
        c0, c1 = Q * s, Q * s + Q
        b0, b1 = tiles[s], tiles[s + 1]
        in0 = (lane >= c0) & (lane < c1)
        in1 = (lane >= c1) & (lane < c1 + Q)
        d0 = [lanes(b0, c0 + m) for m in range(Q)]
        a = [lanes(b1, c0 + m) for m in range(Q)]
        d1 = [lanes(b1, c1 + m) for m in range(Q)]
        v0 = small({(i, m): wide(d0[m][i : i + 1, :]) for m in range(Q) for i in range(m, Q)})
        q, qs = [], []
        for k in range(Q):
            qk = total([a[j] * v0[k, j] for j in range(k + 1)])
            q.append(qk)
            qs.append(spread_rows(qk))
        for m in range(Q):
            d1[m] = d1[m] - total([q[k] * qs[k][m] for k in range(Q)])
        v1 = small({(i, m): wide(d1[m][i : i + 1, :]) for m in range(Q) for i in range(m, Q)})
        t0 = jnp.where(in0, jnp.where(lane - c0 == sub, 1.0, 0.0), jnp.where(in1, 0.0, b0))
        v0t = assemble(lambda i, k: v0[k, i] if i <= k else None)
        w0 = apply(assemble(lambda i, k: v0[i, k] if i >= k else None), spread_rows(t0))
        w0r = spread_rows(w0)
        out.append(jnp.where(lane < c1, w0, 0.0))
        t1 = jnp.where(in0, 0.0, b1) - total([q[k] * w0r[k] for k in range(Q)])
        t1 = jnp.where(in1, jnp.where(lane - c1 == sub, 1.0, 0.0), t1)
        w1 = apply(assemble(lambda i, k: v1[i, k] if i >= k else None), spread_rows(t1))
        out.append(jnp.where(lane < c1 + Q, w1, 0.0))
        if s + 2 < count:
            w1r = spread_rows(w1)
            z1 = apply(assemble(lambda i, k: v1[k, i] if i <= k else None), w1r)
            z1r = spread_rows(z1)
            y = w0 - apply(assemble(lambda i, k: qs[i][k]), z1r)
            zr = spread_rows(apply(v0t, spread_rows(y))) + z1r
            both = in0 | in1
            for t in range(s + 2, count):
                row = tiles[t]
                terms = [lanes(row, c0 + m) * zr[m] for m in range(2 * Q)]
                tiles[t] = jnp.where(both, 0.0, row) - total(terms)
    return out


def factor(load_row, rh, rl, tri, start=None):
    blocks = N // NB
    lane = lax.broadcasted_iota(jnp.int32, (NB, N), 1)
    K0 = ((0,), (0,))
    KM = ((1,), (0,))

    rh[...] = jnp.zeros((N, N), BF16)
    rl[...] = jnp.zeros((N, N), BF16)

    def step(k, carry):
        k0 = pl.multiple_of(k * NB, NB)
        tri[...] = jnp.where(lane >= k0, load_row(k0), 0.0)
        cols = pl.ds(k0, NB)

        def update(p, c):
            rows = pl.ds(pl.multiple_of(p * 2 * NB, 2 * NB), 2 * NB)
            ah, al = rh[rows, cols], rl[rows, cols]
            bh, bl = rh[rows, :], rl[rows, :]
            tri[...] -= dot(ah, bh, K0) + dot(ah, bl, K0) + dot(al, bh, K0)
            return c

        lax.fori_loop(0, (k + 1) // 2, update, 0)
        rh[:, cols] = jnp.zeros((N, NB), BF16)
        rl[:, cols] = jnp.zeros((N, NB), BF16)
        d = tri[:, pl.ds(k0, NB)]
        tiles = diag_inverse([d[Q * i : Q * i + Q, :] for i in range(NB // Q)])
        w = jnp.concatenate(tiles, axis=0)
        tri[:, pl.ds(k0, NB)] = jnp.eye(NB, dtype=F32)
        wh, wl = split(w)
        xh, xl = split(tri[...])
        row = dot(wh, xh, KM) + dot(wh, xl, KM) + dot(wl, xh, KM)
        oh, ol = split(row)
        rh[pl.ds(k0, NB), :] = oh
        rl[pl.ds(k0, NB), :] = ol
        return carry

    lax.fori_loop(0, blocks, step, 0)


def first_kernel(g_ref, oh, ol, tri):
    def load(k0):
        return g_ref[pl.ds(k0, NB), :].astype(F32)

    factor(load, oh, ol, tri)


def second_kernel(where, mine, theirs, w1h, w1l, oh, ol, gh, gl, ch, cl, shifted, tri, bridge, diag):
    KT = ((1,), (1,))
    KM = ((1,), (0,))
    half = 256
    shard = N // where.shape[0]
    for i in range(where.shape[0]):
        at = where[i]
        rows = slice(i * shard, i * shard + shard)
        for base, ref in ((0, mine), (mine.shape[0], theirs)):

            @pl.when((at >= base) & (at < base + ref.shape[0]))
            def _():
                got = ref[jnp.clip(at - base, 0, ref.shape[0] - 1)]
                bridge[rows, :] = got[0:shard]
                diag[rows, :] = got[shard : 2 * shard]

    def couple(i, c):
        rows = pl.ds(pl.multiple_of(i * 2 * half, 2 * half), 2 * half)
        for j in range(N // half):
            t, kk = slice(j * half, j * half + half), half * (j + 1)
            b = bridge[rows, 0:kk]
            hi, lo = split(dot(b, w1h[t, 0:kk], KT) + dot(b, w1l[t, 0:kk], KT))
            ch[rows, t] = hi
            cl[rows, t] = lo
        return c

    lax.fori_loop(0, N // (2 * half), couple, 0)

    def shift(i, c):
        s = pl.ds(pl.multiple_of(i * half, half), half)

        def inner(j, c):
            t = pl.ds(pl.multiple_of(j * half, half), half)
            prod = dot(ch[s, :], ch[t, :], KT) + dot(ch[s, :], cl[t, :], KT) + dot(cl[s, :], ch[t, :], KT)
            shifted[s, t] = diag[s, t].astype(F32) - prod
            return c

        return lax.fori_loop(i, N // half, inner, c)

    lax.fori_loop(0, N // half, shift, 0)
    factor(lambda k0: shifted[pl.ds(k0, NB), :], oh, ol, tri)

    def carry_over(j, c):
        t = pl.ds(pl.multiple_of(j * 2 * half, 2 * half), 2 * half)
        for i in range(N // half):
            s, kk = slice(i * half, i * half + half), half * (i + 1)
            hi, lo = split(
                -(
                    dot(oh[s, 0:kk], ch[0:kk, t], KM)
                    + dot(oh[s, 0:kk], cl[0:kk, t], KM)
                    + dot(ol[s, 0:kk], ch[0:kk, t], KM)
                )
            )
            gh[s, t] = hi
            gl[s, t] = lo
        return c

    lax.fori_loop(0, N // (2 * half), carry_over, 0)


VM = pl.BlockSpec(memory_space=pltpu.VMEM)
LIMIT = 60 * 1024 * 1024


def first_stage(g):
    return pl.pallas_call(
        first_kernel,
        out_shape=[jax.ShapeDtypeStruct((N, N), BF16)] * 2,
        in_specs=[VM],
        out_specs=[VM] * 2,
        scratch_shapes=[pltpu.VMEM((NB, N), F32)],
        compiler_params=pltpu.CompilerParams(vmem_limit_bytes=LIMIT),
        cost_estimate=pl.CostEstimate(flops=10**10, bytes_accessed=10**7, transcendentals=0),
        name="first_stage",
    )(g)


def second_stage(where, mine, theirs, w1h, w1l):
    return pl.pallas_call(
        second_kernel,
        out_shape=[jax.ShapeDtypeStruct((N, N), BF16)] * 4,
        in_specs=[pl.BlockSpec(memory_space=pltpu.SMEM)] + [VM] * 4,
        out_specs=[VM] * 4,
        scratch_shapes=[pltpu.VMEM((N, N), BF16)] * 2
        + [pltpu.VMEM((N, N), F32)]
        + [pltpu.VMEM((NB, N), F32)]
        + [pltpu.VMEM((N, N), BF16)] * 2,
        compiler_params=pltpu.CompilerParams(vmem_limit_bytes=LIMIT),
        cost_estimate=pl.CostEstimate(flops=2 * 10**10, bytes_accessed=10**7, transcendentals=0),
        name="second_stage",
    )(where, mine, theirs, w1h, w1l)


PER, GROUP = 2, 4
HALF = 256


def solve_tiles(src, w1h, w1l, w2h, w2l, gh, gl, put):
    KT = ((1,), (1,))
    p1 = jnp.concatenate([src[u, 0] for u in range(PER)], axis=0)
    p2 = jnp.concatenate([src[u, 1] for u in range(PER)], axis=0)
    parts = []
    for j in range(N // HALF):
        t, kk = slice(j * HALF, j * HALF + HALF), HALF * (j + 1)
        got = dot(p1[:, 0:kk], w1h[t, 0:kk], KT) + dot(p1[:, 0:kk], w1l[t, 0:kk], KT)
        parts.append(got.astype(BF16))
        put(j * HALF, parts[-1])
    l1 = jnp.concatenate(parts, axis=1)
    for j in range(N // HALF):
        t, kk = slice(j * HALF, j * HALF + HALF), HALF * (j + 1)
        got = dot(p2[:, 0:kk], w2h[t, 0:kk], KT) + dot(p2[:, 0:kk], w2l[t, 0:kk], KT)
        got = got + dot(l1, gh[t, :], KT) + dot(l1, gl[t, :], KT)
        put(N + j * HALF, got.astype(BF16))


def rows_kernel(need, own, src, w1h, w1l, w2h, w2l, gh, gl, own_first, own_second, out):
    step = pl.program_id(0)

    @pl.when(need[step] > 0)
    def _():
        def put(c, val):
            for u in range(PER):
                out[u, :, c : c + HALF] = val[u * HALF : u * HALF + HALF, :]

        solve_tiles(src, w1h, w1l, w2h, w2l, gh, gl, put)

    for u in range(PER):

        @pl.when(own[0] == step * PER + u)
        def _():
            own_first[0] = out[u, :, 0:N]
            own_second[0] = out[u, :, N : 2 * N]


ONCE = pl.BlockSpec((N, N), lambda s, *_: (0, 0), pipeline_mode=pl.Buffered(1))


def rows_stage(need, own, src, weights):
    count = src.shape[0]
    own_spec = pl.BlockSpec((1, HALF, N), lambda s, *_: (0, 0, 0))
    return pl.pallas_call(
        rows_kernel,
        out_shape=[
            jax.ShapeDtypeStruct((1, HALF, N), BF16),
            jax.ShapeDtypeStruct((1, HALF, N), BF16),
            jax.ShapeDtypeStruct((count, HALF, 2 * N), BF16),
        ],
        grid_spec=pltpu.PrefetchScalarGridSpec(
            num_scalar_prefetch=2,
            grid=(count // PER,),
            in_specs=[pl.BlockSpec((PER, 2, HALF, N), lambda s, *_: (s, 0, 0, 0))] + [ONCE] * 6,
            out_specs=[own_spec, own_spec, pl.BlockSpec((PER, HALF, 2 * N), lambda s, *_: (s, 0, 0))],
        ),
        compiler_params=pltpu.CompilerParams(vmem_limit_bytes=LIMIT, dimension_semantics=("arbitrary",)),
        cost_estimate=pl.CostEstimate(flops=4 * 10**10, bytes_accessed=4 * 10**7, transcendentals=0),
        name="rows_stage",
    )(need, own, src, *weights)


def final_kernel(pairs, live, need, src, w1h, w1l, w2h, w2l, gh, gl, rows, tin, tout, lcol, lrow, sem):
    KT = ((1,), (1,))
    step = pl.program_id(0)
    ncol = lcol.shape[0] // PER
    fetch = pltpu.make_async_copy(rows, lrow, sem)

    @pl.when(step == 0)
    def _():
        fetch.start()

    @pl.when(step < ncol)
    def _():
        at = jnp.minimum(step, ncol - 1)

        @pl.when(need[at] > 0)
        def _():
            def put(c, val):
                for u in range(PER):
                    lcol[at * PER + u, :, c : c + HALF] = val[u * HALF : u * HALF + HALF, :]

            solve_tiles(src, w1h, w1l, w2h, w2l, gh, gl, put)

    @pl.when(step == ncol)
    def _():
        fetch.wait()

    @pl.when(step >= ncol)
    def _():
        base = (step - ncol) * GROUP
        for u in range(GROUP):
            slot = base + u

            @pl.when(slot < live[0])
            def _():
                a, b = pairs[slot], pairs[24 + slot]
                tout[0, u] = tin[0, u] - dot(lrow[a], lcol[b], KT)

            @pl.when(slot >= live[0])
            def _():
                tout[0, u] = tin[0, u]


def final_stage(pairs, live, need, src, weights, rows, trailing):
    count, slots = src.shape[0], trailing.shape[1]
    cs, ks = count // PER, slots // GROUP
    tmap = lambda s, *_: (0, jnp.clip(s - cs, 0, ks - 1), 0, 0)
    return pl.pallas_call(
        final_kernel,
        out_shape=jax.ShapeDtypeStruct(trailing.shape, F32),
        grid_spec=pltpu.PrefetchScalarGridSpec(
            num_scalar_prefetch=3,
            grid=(cs + ks,),
            in_specs=[pl.BlockSpec((PER, 2, HALF, N), lambda s, *_: (jnp.minimum(s, cs - 1), 0, 0, 0))]
            + [ONCE] * 6
            + [pl.BlockSpec(memory_space=pl.ANY), pl.BlockSpec((1, GROUP, HALF, HALF), tmap)],
            out_specs=pl.BlockSpec((1, GROUP, HALF, HALF), tmap),
            scratch_shapes=[
                pltpu.VMEM((count, HALF, 2 * N), BF16),
                pltpu.VMEM(rows.shape, BF16),
                pltpu.SemaphoreType.DMA,
            ],
        ),
        compiler_params=pltpu.CompilerParams(vmem_limit_bytes=LIMIT, dimension_semantics=("arbitrary",)),
        cost_estimate=pl.CostEstimate(flops=3 * 10**10, bytes_accessed=4 * 10**7, transcendentals=0),
        name="final_stage",
    )(pairs, live, need, src, *weights, rows, trailing)


def spread(x, nrow, ncol):
    every = [(r, c) for r in range(nrow) for c in range(ncol)]
    half = ncol // 2
    flat = lambda r, c: r % nrow * ncol + c % ncol
    near, away = (
        lax.ppermute(x, ("row", "col"), [(flat(r, c + r + off), flat(r, c)) for r, c in every])
        for off in (0, half)
    )
    unit = jnp.stack([near, away], axis=0)
    up = lax.ppermute(unit, "row", [(r, (r + 2) % nrow) for r in range(nrow)])
    down = lax.ppermute(unit, "row", [(r, (r - 2) % nrow) for r in range(nrow)])
    row, col = lax.axis_index("row"), lax.axis_index("col")
    core = row % 2
    far = lax.ppermute(
        jnp.where(core == 0, up, down), "row", [(r, (r + (2 if r % 2 == 0 else -2)) % nrow) for r in range(nrow)]
    )
    mine = jnp.concatenate([unit, down, far, up], axis=0)
    theirs = lax.ppermute(mine, "row", [(r, r ^ 1) for r in range(nrow)])
    off = (jnp.arange(ncol, dtype=jnp.int32) - col) % ncol
    holder, side = off % half, off // half
    ahead = (holder // 2 - row // 2) % (nrow // 2)
    other = (holder % 2 != core).astype(jnp.int32)
    return mine, theirs, (other * mine.shape[0] + 2 * ahead + side).astype(jnp.int32)


def per_device(
    nrow, ncol, panel_first, panel_second, diag_first, bridge, diag_second, trailing, trail_pairs, live_count
):
    whole_first = lax.all_gather(diag_first, "col", axis=0, tiled=True)
    mine, theirs, where = spread(jnp.concatenate([bridge, diag_second], axis=0), nrow, ncol)
    both = jnp.stack([panel_first[0], panel_second[0]], axis=0)
    row_p = lax.all_gather(both, "col", axis=0)
    col_p = lax.all_gather(both, "row", axis=0)
    own = lax.axis_index("col").astype(jnp.int32)
    pairs = trail_pairs[0]
    active = jnp.arange(pairs.shape[1], dtype=jnp.int32) < live_count[0]
    group_r = jnp.arange(ncol // PER, dtype=jnp.int32)
    group_c = jnp.arange(nrow // PER, dtype=jnp.int32)
    need_row = jnp.any((pairs[0][None] // PER == group_r[:, None]) & active[None], axis=1) | (group_r == own // PER)
    need_col = jnp.any((pairs[1][None] // PER == group_c[:, None]) & active[None], axis=1)
    w1h, w1l = first_stage(whole_first)
    weights = (w1h, w1l, *second_stage(where, mine, theirs, w1h, w1l))
    lower_first, lower_second, rows = rows_stage(need_row.astype(jnp.int32), own[None], row_p, weights)
    owned = final_stage(pairs.reshape(-1), live_count, need_col.astype(jnp.int32), col_p, weights, rows, trailing)
    return lower_first, lower_second, owned


def solution(mesh):
    return jax.shard_map(
        functools.partial(per_device, mesh.shape["row"], mesh.shape["col"]),
        mesh=mesh,
        in_specs=(
            P(("row", "col"), None, None),
            P(("row", "col"), None, None),
            P("col", None),
            P("col", None),
            P("col", None),
            P(("row", "col"), None, None, None),
            P(("row", "col"), None, None),
            P(("row", "col")),
        ),
        out_specs=(
            P(("row", "col"), None, None),
            P(("row", "col"), None, None),
            P(("row", "col"), None, None, None),
        ),
        check_vma=False,
    )
```

profile of v0, /device:TPU:0, one launch (start us, length us, event | category | flops | bytes accessed | tf_op | source)
XLA Modules:
  0.0 269.7 jit_solution(2136333635311887479)
XLA Ops:
  7.2 0.7 all-gather.6.cloned.1.call-update
  8.0 1.1 constant_dynamic-update-slice_fusion.1
  9.1 1.1 constant_dynamic-update-slice_fusion
  10.2 1.0 copy-done
  11.2 0.0 all-gather.10.cloned.1.call-start
  11.3 0.7 all-gather.10.cloned.1.call-update
  12.0 0.7 collective-permute-start
  12.7 3.4 %collective-permute-start.1 = (bf16[128,1024]{1,0:T(8,128)(2,1)S(1)}, bf16[128,1024]{1,0:T(8,128)(2,1)S(1)}, u32[]{:S(2)}, u32[]{:S(2)}) collective-permute-start(bf16[128,1024]{1,0:T(8,128)(2,1)S(1)} %constant_dynamic-update-slice_fusion.2), channel_id=1, source_target_pairs={{8,0},{9,1},{10,2},{11,3},{12,4},{13,5},{14,6},{15,7},{0,8},{1,9},... | collective-permute-start | bytes 786440 | tf_op jit(solution)/shard_map/ppermute | solution.py:389
  16.1 4.6 %collective-permute-done.1 = bf16[128,1024]{1,0:T(8,128)(2,1)S(1)} collective-permute-done((bf16[128,1024]{1,0:T(8,128)(2,1)S(1)}, bf16[128,1024]{1,0:T(8,128)(2,1)S(1)}, u32[]{:S(2)}, u32[]{:S(2)}) %collective-permute-start.1) | collective-permute-done | bytes 262176 | tf_op jit(solution)/shard_map/ppermute | solution.py:389
  20.6 0.1 pad_maximum_fusion
  20.7 15.2 %collective-permute-start.3 = (bf16[2,128,1024]{2,1,0:T(8,128)(2,1)S(1)}, bf16[2,128,1024]{2,1,0:T(8,128)(2,1)S(1)}, u32[]{:S(2)}, u32[]{:S(2)}) collective-permute-start(bf16[2,128,1024]{2,1,0:T(8,128)(2,1)S(1)} %pad_maximum_fusion), channel_id=1, source_target_pairs={{0,32},{16,48},{32,64},{48,80},{64,96},{80,112},{96,0},{112,16},{1... | collective-permute-start | bytes 1572872 | tf_op jit(solution)/shard_map/ppermute | solution.py:393
  35.8 2.9 %collective-permute-start.2 = (bf16[2,128,1024]{2,1,0:T(8,128)(2,1)S(1)}, bf16[2,128,1024]{2,1,0:T(8,128)(2,1)S(1)}, u32[]{:S(2)}, u32[]{:S(2)}) collective-permute-start(bf16[2,128,1024]{2,1,0:T(8,128)(2,1)S(1)} %pad_maximum_fusion), channel_id=1, source_target_pairs={{0,96},{16,112},{32,0},{48,16},{64,32},{80,48},{96,64},{112,80},{1... | collective-permute-start | bytes 1572872 | tf_op jit(solution)/shard_map/ppermute | solution.py:394
  38.7 0.7 constant_dynamic-update-slice_fusion.8
  39.4 0.7 constant_dynamic-update-slice_fusion.7
  40.2 7.1 %collective-permute-done.3 = bf16[2,128,1024]{2,1,0:T(8,128)(2,1)S(1)} collective-permute-done((bf16[2,128,1024]{2,1,0:T(8,128)(2,1)S(1)}, bf16[2,128,1024]{2,1,0:T(8,128)(2,1)S(1)}, u32[]{:S(2)}, u32[]{:S(2)}) %collective-permute-start.3) | collective-permute-done | bytes 524320 | tf_op jit(solution)/shard_map/ppermute | solution.py:393
  47.2 1.0 broadcast_select_fusion
  48.3 1.9 collective-permute-start.4
  50.1 8.5 %collective-permute-done.4 = bf16[2,128,1024]{2,1,0:T(8,128)(2,1)S(1)} collective-permute-done((bf16[2,128,1024]{2,1,0:T(8,128)(2,1)S(1)}, bf16[2,128,1024]{2,1,0:T(8,128)(2,1)S(1)}, u32[]{:S(2)}, u32[]{:S(2)}) %collective-permute-start.4) | collective-permute-done | bytes 524320 | tf_op jit(solution)/shard_map/ppermute | solution.py:397
  58.7 0.8 constant_dynamic-update-slice_fusion.5
  59.5 0.8 constant_dynamic-update-slice_fusion.4.mine
  61.0 0.7 reshape_squeeze.3.pairs
  61.7 0.1 fusion.3
  61.8 0.6 convert_element_type.8.need
  62.4 0.5 fusion.5.where
  62.9 0.1 fusion.1
  63.0 0.5 or_convert_fusion.need
  63.5 40.0 %first_stage.1 = (bf16[1024,1024]{1,0:T(8,128)(2,1)}, bf16[1024,1024]{1,0:T(8,128)(2,1)}) custom-call(bf16[1024,1024]{1,0:T(8,128)(2,1)} %all-gather.6.cloned.1.call-done.g_ref), custom_call_target="tpu_custom_call" | custom-call | flops 10000000000 | bytes 10000000 | tf_op jit(solution)/shard_map/first_stage/pallas_call | solution.py:222
  103.5 56.2 %second_stage.1 = (bf16[1024,1024]{1,0:T(8,128)(2,1)}, bf16[1024,1024]{1,0:T(8,128)(2,1)}, bf16[1024,1024]{1,0:T(8,128)(2,1)}, bf16[1024,1024]{1,0:T(8,128)(2,1)}) custom-call(s32[16]{0:T(128)} %fusion.5.where, bf16[8,128,1024]{2,1,0:T(8,128)(2,1)} %constant_dynamic-update-slice_fusion.4.mine, bf16[8,128,1024]{2,1,0:T(8,128)(2,1)} %collective-permute-done.5.theirs, ...), custom_call_target="tpu_custom_call" | custom-call | flops 20000000000 | bytes 10000000 | tf_op jit(solution)/shard_map/second_stage/pallas_call | solution.py:235
  159.8 12.1 %all-gather.8.cloned.1.call-done = bf16[32,256,1024]{2,1,0:T(8,128)(2,1)} async-done(((bf16[2,256,1024]{2,1,0:T(8,128)(2,1)}), bf16[32,256,1024]{2,1,0:T(8,128)(2,1)}) %all-gather.8.cloned.1.call-update) | async-done | bytes 16777232 | tf_op jit(solution)/shard_map/all_gather | solution.py:415
  171.9 48.7 %rows_stage.1 = (bf16[1,256,1024]{2,1,0:T(8,128)(2,1)}, bf16[1,256,1024]{2,1,0:T(8,128)(2,1)}, bf16[16,256,2048]{2,1,0:T(8,128)(2,1)}) custom-call(s32[8]{0:T(128)} %or_convert_fusion.need, s32[1]{0:T(128)} %bitcast.2.own, bf16[16,2,256,1024]{3,2,1,0:T(8,128)(2,1)} %bitcast.27, bf16[1024,1024]{1,0:T(8,128)(2,1)} %get-tuple-element.12.w1h, ...), custom_call_target="tpu_custom_call" | custom-call | flops 40000000000 | bytes 40000000 | tf_op jit(solution)/shard_map/rows_stage/pallas_call | solution.py:297
  220.6 2.7 all-gather.10.cloned.1.call-done
  223.2 39.9 %final_stage.1 = f32[1,24,256,256]{3,2,1,0:T(8,128)} custom-call(s32[48]{0:T(128)} %reshape_squeeze.3.pairs, s32[1]{0:T(128)} %copy.17.live, s32[4]{0:T(128)} %convert_element_type.8.need, bf16[8,2,256,1024]{3,2,1,0:T(8,128)(2,1)} %bitcast.28, bf16[1024,1024]{1,0:T(8,128)(2,1)} %get-tuple-element.12.w1h, bf16[1024,1024]{1,0:T(8,128)(2,1)} %get-tuple-element.13.w1l, ...), custom_call_target="tpu_custom_call" | custom-call | flops 30000001024 | bytes 40000000 | tf_op jit(solution)/shard_map/final_stage/pallas_call | solution.py:362
  (19 shorter events, 0.2 us)
Async XLA Ops:
  7.2 56.4 %all-gather.6.cloned.1.call-start = ((), (), s32[]{:S(2)}) async-start(), calls=%async_computation | async-start | bytes 2228224 | tf_op jit(solution)/shard_map/all_gather | solution.py:412
  7.9 4.0 %copy-start.1 = (bf16[64,1024]{1,0:T(8,128)(2,1)S(1)}, bf16[64,1024]{1,0:T(8,128)(2,1)}, u32[]{:S(2)}) copy-start(bf16[64,1024]{1,0:T(8,128)(2,1)} %param.11) | copy-start | bytes 393220
  7.9 4.1 %copy-start.2 = (bf16[64,1024]{1,0:T(8,128)(2,1)S(1)}, bf16[64,1024]{1,0:T(8,128)(2,1)}, u32[]{:S(2)}) copy-start(bf16[64,1024]{1,0:T(8,128)(2,1)} %param.12) | copy-start | bytes 393220
  7.9 164.0 %all-gather.8.cloned.1.call-start = ((), (), s32[]{:S(2)}) async-start(), calls=%async_computation.1 | async-start | bytes 17825792 | tf_op jit(solution)/shard_map/all_gather | solution.py:415
  10.2 1.0 copy-start
  11.2 212.0 %all-gather.10.cloned.1.call-start = ((), (), s32[]{:S(2)}) async-start(), calls=%async_computation.2 | async-start | bytes 9437184 | tf_op jit(solution)/shard_map/all_gather | solution.py:416
  12.0 4.1 %collective-permute-start = (bf16[128,1024]{1,0:T(8,128)(2,1)S(1)}, bf16[128,1024]{1,0:T(8,128)(2,1)S(1)}, u32[]{:S(2)}, u32[]{:S(2)}) collective-permute-start(bf16[128,1024]{1,0:T(8,128)(2,1)S(1)} %constant_dynamic-update-slice_fusion.2), channel_id=1, source_target_pairs={{0,0},{1,1},{2,2},{3,3},{4,4},{5,5},{6,6},{7,7},{8,8},{9,9},{10,10... | collective-permute-start | bytes 786440 | tf_op jit(solution)/shard_map/ppermute | solution.py:389
  12.7 7.9 %collective-permute-start.1 = (bf16[128,1024]{1,0:T(8,128)(2,1)S(1)}, bf16[128,1024]{1,0:T(8,128)(2,1)S(1)}, u32[]{:S(2)}, u32[]{:S(2)}) collective-permute-start(bf16[128,1024]{1,0:T(8,128)(2,1)S(1)} %constant_dynamic-update-slice_fusion.2), channel_id=1, source_target_pairs={{8,0},{9,1},{10,2},{11,3},{12,4},{13,5},{14,6},{15,7},{0,8},{1,9},... | collective-permute-start | bytes 786440 | tf_op jit(solution)/shard_map/ppermute | solution.py:389
  20.7 26.6 %collective-permute-start.3 = (bf16[2,128,1024]{2,1,0:T(8,128)(2,1)S(1)}, bf16[2,128,1024]{2,1,0:T(8,128)(2,1)S(1)}, u32[]{:S(2)}, u32[]{:S(2)}) collective-permute-start(bf16[2,128,1024]{2,1,0:T(8,128)(2,1)S(1)} %pad_maximum_fusion), channel_id=1, source_target_pairs={{0,32},{16,48},{32,64},{48,80},{64,96},{80,112},{96,0},{112,16},{1... | collective-permute-start | bytes 1572872 | tf_op jit(solution)/shard_map/ppermute | solution.py:393
  35.8 11.4 %collective-permute-start.2 = (bf16[2,128,1024]{2,1,0:T(8,128)(2,1)S(1)}, bf16[2,128,1024]{2,1,0:T(8,128)(2,1)S(1)}, u32[]{:S(2)}, u32[]{:S(2)}) collective-permute-start(bf16[2,128,1024]{2,1,0:T(8,128)(2,1)S(1)} %pad_maximum_fusion), channel_id=1, source_target_pairs={{0,96},{16,112},{32,0},{48,16},{64,32},{80,48},{96,64},{112,80},{1... | collective-permute-start | bytes 1572872 | tf_op jit(solution)/shard_map/ppermute | solution.py:394
  40.2 20.8 %copy-start.3 = (s32[1,2,24]{2,1,0:T(2,128)S(1)}, s32[1,2,24]{2,1,0:T(2,128)}, u32[]{:S(2)}) copy-start(s32[1,2,24]{2,1,0:T(2,128)} %param.14) | copy-start | bytes 580
  48.3 10.4 %collective-permute-start.4 = (bf16[2,128,1024]{2,1,0:T(8,128)(2,1)S(1)}, bf16[2,128,1024]{2,1,0:T(8,128)(2,1)S(1)}, u32[]{:S(2)}, u32[]{:S(2)}) collective-permute-start(bf16[2,128,1024]{2,1,0:T(8,128)(2,1)S(1)} %get-tuple-element.21), channel_id=1, source_target_pairs={{0,32},{16,112},{32,64},{48,16},{64,96},{80,48},{96,0},{112,80},{1... | collective-permute-start | bytes 1572872 | tf_op jit(solution)/shard_map/ppermute | solution.py:397
  60.3 43.2 %collective-permute-start.5 = (bf16[8,128,1024]{2,1,0:T(8,128)(2,1)}, bf16[8,128,1024]{2,1,0:T(8,128)(2,1)}, u32[]{:S(2)}, u32[]{:S(2)}) collective-permute-start(bf16[8,128,1024]{2,1,0:T(8,128)(2,1)} %constant_dynamic-update-slice_fusion.4.mine), channel_id=1, source_target_pairs={{0,16},{16,0},{32,48},{48,32},{64,80},{80,64},{96,112},{112,96},{1... | collective-permute-start | bytes 6291464 | tf_op jit(solution)/shard_map/ppermute | solution.py:401
Sparse Core Ops, SparseCore 0:
  10.1 49.1 all-gather.5
  61.4 110.4 all-gather.7
  173.6 49.5 all-gather.9
where the time goes:
time: 270 us
  Pallas kernels  185 us (69%)
  waiting for transfers between devices  36.4 us (13%)
  starting transfers between devices  24.1 us (9%)
  between operations  14.5 us (5%)
  local copies, waits for them, and re-layouts  6.98 us (3%)
  other arithmetic  2.96 us (1%)
    pallas_call x1, Pallas kernels, second_stage(): pl.pallas_call(second_kernel, out_shape=[jax.ShapeDtypeStruct((N, N), BF1...  56.2 us
    pallas_call x1, Pallas kernels, rows_stage(): pl.pallas_call(rows_kernel, out_shape=[jax.ShapeDtypeStruct((1, HALF, N),...  48.7 us
    pallas_call x1, Pallas kernels, first_stage(): pl.pallas_call(first_kernel, out_shape=[jax.ShapeDtypeStruct((N, N), BF16...  40 us
    pallas_call x1, Pallas kernels, final_stage(): pl.pallas_call(final_kernel, out_shape=jax.ShapeDtypeStruct(trailing.shap...  39.9 us
    ppermute x1, starting transfers between devices, spread(): up = lax.ppermute(unit, 'row', [(r, (r + 2) % nrow) for r in range(nrow)])  15.2 us
    all_gather x1, waiting for transfers between devices, per_device(): row_p = lax.all_gather(both, 'col', axis=0)  12.1 us
    ppermute x1, waiting for transfers between devices, spread(): lax.ppermute(jnp.where(core == 0, up, down), 'row', [(r, (r + (2 if r % 2...  8.54 us
    ppermute x1, waiting for transfers between devices, spread(): up = lax.ppermute(unit, 'row', [(r, (r + 2) % nrow) for r in range(nrow)])  7.08 us
  transfers between devices with their start and end apart: 9, of which 5 were waited for; matrix products, arithmetic and copies ran while one was open for 3% of the time, Pallas kernels for 54%

commit v1 on v0

--- a/solution.py
+++ b/solution.py
@@ -247,7 +247,7 @@
     )(where, mine, theirs, w1h, w1l)
 
 
-PER, GROUP = 2, 4
+PER, GROUP, SLOTS = 2, 4, 24
 HALF = 256
 
 
@@ -269,85 +269,125 @@
         put(N + j * HALF, got.astype(BF16))
 
 
-def rows_kernel(need, own, src, w1h, w1l, w2h, w2l, gh, gl, own_first, own_second, out):
+ONCE = pl.BlockSpec((N, N), lambda s, *_: (0, 0), pipeline_mode=pl.Buffered(1))
+ANY = pl.BlockSpec(memory_space=pl.ANY)
+
+
+def put_into(ref, base):
+    def put(c, val):
+        for u in range(PER):
+            ref[base + u, :, c : c + HALF] = val[u * HALF : u * HALF + HALF, :]
+
+    return put
+
+
+def cols_kernel(a0, a1, a2, a3, w1h, w1l, w2h, w2l, gh, gl, own_first, own_second, out, buf, sems):
     step = pl.program_id(0)
-
-    @pl.when(need[step] > 0)
-    def _():
-        def put(c, val):
-            for u in range(PER):
-                out[u, :, c : c + HALF] = val[u * HALF : u * HALF + HALF, :]
-
-        solve_tiles(src, w1h, w1l, w2h, w2l, gh, gl, put)
-
-    for u in range(PER):
-
-        @pl.when(own[0] == step * PER + u)
-        def _():
-            own_first[0] = out[u, :, 0:N]
-            own_second[0] = out[u, :, N : 2 * N]
-
-
-ONCE = pl.BlockSpec((N, N), lambda s, *_: (0, 0), pipeline_mode=pl.Buffered(1))
-
-
-def rows_stage(need, own, src, weights):
-    count = src.shape[0]
+    copies = [pltpu.make_async_copy(a, buf.at[i], sems.at[i]) for i, a in enumerate((a0, a1, a2, a3))]
+
+    @pl.when(step == 0)
+    def _():
+        for copy in copies:
+            copy.start()
+        for copy in copies[:PER]:
+            copy.wait()
+
+    @pl.when(step == 1)
+    def _():
+        for copy in copies[PER:]:
+            copy.wait()
+
+    solve_tiles(buf.at[pl.ds(step * PER, PER)], w1h, w1l, w2h, w2l, gh, gl, put_into(out, 0))
+
+    @pl.when(step == 0)
+    def _():
+        own_first[0] = out[0, :, 0:N]
+        own_second[0] = out[0, :, N : 2 * N]
+
+
+def cols_stage(arrays, weights):
+    count = len(arrays)
     own_spec = pl.BlockSpec((1, HALF, N), lambda s, *_: (0, 0, 0))
     return pl.pallas_call(
-        rows_kernel,
+        cols_kernel,
         out_shape=[
             jax.ShapeDtypeStruct((1, HALF, N), BF16),
             jax.ShapeDtypeStruct((1, HALF, N), BF16),
             jax.ShapeDtypeStruct((count, HALF, 2 * N), BF16),
         ],
+        grid=(count // PER,),
+        in_specs=[ANY] * count + [ONCE] * 6,
+        out_specs=[own_spec, own_spec, pl.BlockSpec((PER, HALF, 2 * N), lambda s: (s, 0, 0))],
+        scratch_shapes=[pltpu.VMEM((count, 2, HALF, N), BF16), pltpu.SemaphoreType.DMA((count,))],
+        compiler_params=pltpu.CompilerParams(vmem_limit_bytes=LIMIT, dimension_semantics=("arbitrary",)),
+        cost_estimate=pl.CostEstimate(flops=10**10, bytes_accessed=3 * 10**7, transcendentals=0),
+        name="cols_stage",
+    )(*arrays, *weights)
+
+
+def rows_kernel(need, src, w1h, w1l, w2h, w2l, gh, gl, out):
+    @pl.when(need[pl.program_id(0)] > 0)
+    def _():
+        solve_tiles(src, w1h, w1l, w2h, w2l, gh, gl, put_into(out, 0))
+
+
+def rows_stage(need, src, weights):
+    count = src.shape[0] // 2
+    return pl.pallas_call(
+        rows_kernel,
+        out_shape=jax.ShapeDtypeStruct((count, HALF, 2 * N), BF16),
         grid_spec=pltpu.PrefetchScalarGridSpec(
-            num_scalar_prefetch=2,
+            num_scalar_prefetch=1,
             grid=(count // PER,),
             in_specs=[pl.BlockSpec((PER, 2, HALF, N), lambda s, *_: (s, 0, 0, 0))] + [ONCE] * 6,
-            out_specs=[own_spec, own_spec, pl.BlockSpec((PER, HALF, 2 * N), lambda s, *_: (s, 0, 0))],
+            out_specs=pl.BlockSpec((PER, HALF, 2 * N), lambda s, *_: (s, 0, 0)),
         ),
         compiler_params=pltpu.CompilerParams(vmem_limit_bytes=LIMIT, dimension_semantics=("arbitrary",)),
-        cost_estimate=pl.CostEstimate(flops=4 * 10**10, bytes_accessed=4 * 10**7, transcendentals=0),
+        cost_estimate=pl.CostEstimate(flops=2 * 10**10, bytes_accessed=4 * 10**7, transcendentals=0),
         name="rows_stage",
-    )(need, own, src, *weights)
-
-
-def final_kernel(pairs, live, need, src, w1h, w1l, w2h, w2l, gh, gl, rows, tin, tout, lcol, lrow, sem):
+    )(need, src, *weights)
+
+
+def final_kernel(
+    pairs, live, need, src, w1h, w1l, w2h, w2l, gh, gl, done_rows, mine, theirs, tin, tout, lcol, lrow, sems
+):
     KT = ((1,), (1,))
     step = pl.program_id(0)
-    ncol = lcol.shape[0] // PER
-    fetch = pltpu.make_async_copy(rows, lrow, sem)
+    first, side = done_rows.shape[0], mine.shape[0]
+    steps = (lrow.shape[0] - first) // PER
+    copies = [
+        pltpu.make_async_copy(done_rows, lrow.at[pl.ds(0, first)], sems.at[0]),
+        pltpu.make_async_copy(mine, lcol.at[pl.ds(0, side)], sems.at[1]),
+        pltpu.make_async_copy(theirs, lcol.at[pl.ds(side, side)], sems.at[2]),
+    ]
 
     @pl.when(step == 0)
     def _():
-        fetch.start()
-
-    @pl.when(step < ncol)
-    def _():
-        at = jnp.minimum(step, ncol - 1)
-
-        @pl.when(need[at] > 0)
+        for copy in copies:
+            copy.start()
+
+    @pl.when(step < steps)
+    def _():
+        at = jnp.minimum(step, steps - 1)
+
+        @pl.when(need[steps + at] > 0)
         def _():
-            def put(c, val):
-                for u in range(PER):
-                    lcol[at * PER + u, :, c : c + HALF] = val[u * HALF : u * HALF + HALF, :]
-
-            solve_tiles(src, w1h, w1l, w2h, w2l, gh, gl, put)
-
-    @pl.when(step == ncol)
-    def _():
-        fetch.wait()
-
-    @pl.when(step >= ncol)
-    def _():
-        base = (step - ncol) * GROUP
+            solve_tiles(src, w1h, w1l, w2h, w2l, gh, gl, put_into(lrow, first + at * PER))
+
+    @pl.when(step == steps)
+    def _():
+        for copy in copies:
+            copy.wait()
+
+    @pl.when(step >= steps)
+    def _():
+        base = (step - steps) * GROUP
         for u in range(GROUP):
             slot = base + u
 
             @pl.when(slot < live[0])
             def _():
-                a, b = pairs[slot], pairs[24 + slot]
+                a, b = pairs[slot], pairs[SLOTS + slot]
                 tout[0, u] = tin[0, u] - dot(lrow[a], lcol[b], KT)
 
             @pl.when(slot >= live[0])
@@ -355,9 +395,9 @@
                 tout[0, u] = tin[0, u]
 
 
-def final_stage(pairs, live, need, src, weights, rows, trailing):
+def final_stage(pairs, live, need, src, weights, done_rows, mine, theirs, trailing):
     count, slots = src.shape[0], trailing.shape[1]
-    cs, ks = count // PER, slots // GROUP
+    cs, ks = done_rows.shape[0] // PER, slots // GROUP
     tmap = lambda s, *_: (0, jnp.clip(s - cs, 0, ks - 1), 0, 0)
     return pl.pallas_call(
         final_kernel,
@@ -365,20 +405,21 @@
         grid_spec=pltpu.PrefetchScalarGridSpec(
             num_scalar_prefetch=3,
             grid=(cs + ks,),
-            in_specs=[pl.BlockSpec((PER, 2, HALF, N), lambda s, *_: (jnp.minimum(s, cs - 1), 0, 0, 0))]
+            in_specs=[pl.BlockSpec((PER, 2, HALF, N), lambda s, *_: (cs + jnp.minimum(s, cs - 1), 0, 0, 0))]
             + [ONCE] * 6
-            + [pl.BlockSpec(memory_space=pl.ANY), pl.BlockSpec((1, GROUP, HALF, HALF), tmap)],
+            + [ANY] * 3
+            + [pl.BlockSpec((1, GROUP, HALF, HALF), tmap)],
             out_specs=pl.BlockSpec((1, GROUP, HALF, HALF), tmap),
             scratch_shapes=[
+                pltpu.VMEM((2 * mine.shape[0], HALF, 2 * N), BF16),
                 pltpu.VMEM((count, HALF, 2 * N), BF16),
-                pltpu.VMEM(rows.shape, BF16),
-                pltpu.SemaphoreType.DMA,
+                pltpu.SemaphoreType.DMA((3,)),
             ],
         ),
         compiler_params=pltpu.CompilerParams(vmem_limit_bytes=LIMIT, dimension_semantics=("arbitrary",)),
         cost_estimate=pl.CostEstimate(flops=3 * 10**10, bytes_accessed=4 * 10**7, transcendentals=0),
         name="final_stage",
-    )(pairs, live, need, src, *weights, rows, trailing)
+    )(pairs, live, need, src, *weights, done_rows, mine, theirs, trailing)
 
 
 def spread(x, nrow, ncol):
@@ -413,18 +454,24 @@
     mine, theirs, where = spread(jnp.concatenate([bridge, diag_second], axis=0), nrow, ncol)
     both = jnp.stack([panel_first[0], panel_second[0]], axis=0)
     row_p = lax.all_gather(both, "col", axis=0)
-    col_p = lax.all_gather(both, "row", axis=0)
-    own = lax.axis_index("col").astype(jnp.int32)
+    held, mine = lax.optimization_barrier((both, mine))
+    up, down, far = (
+        lax.ppermute(held, "row", [(r, (r + d) % nrow) for r in range(nrow)]) for d in (2, -2, nrow // 2)
+    )
+    row = lax.axis_index("row")
     pairs = trail_pairs[0]
+    seat = 4 * (pairs[1] % 2 != row % 2).astype(jnp.int32) + (pairs[1] // 2 - row // 2) % (nrow // 2)
     active = jnp.arange(pairs.shape[1], dtype=jnp.int32) < live_count[0]
-    group_r = jnp.arange(ncol // PER, dtype=jnp.int32)
-    group_c = jnp.arange(nrow // PER, dtype=jnp.int32)
-    need_row = jnp.any((pairs[0][None] // PER == group_r[:, None]) & active[None], axis=1) | (group_r == own // PER)
-    need_col = jnp.any((pairs[1][None] // PER == group_c[:, None]) & active[None], axis=1)
+    group = jnp.arange(ncol // PER, dtype=jnp.int32)
+    need = jnp.any((pairs[0][None] // PER == group[:, None]) & active[None], axis=1).astype(jnp.int32)
     w1h, w1l = first_stage(whole_first)
     weights = (w1h, w1l, *second_stage(where, mine, theirs, w1h, w1l))
-    lower_first, lower_second, rows = rows_stage(need_row.astype(jnp.int32), own[None], row_p, weights)
-    owned = final_stage(pairs.reshape(-1), live_count, need_col.astype(jnp.int32), col_p, weights, rows, trailing)
+    lower_first, lower_second, ours = cols_stage((held, down, far, up), weights)
+    others = lax.ppermute(ours, "row", [(r, r ^ 1) for r in range(nrow)])
+    done_rows = rows_stage(need, row_p, weights)
+    owned = final_stage(
+        jnp.concatenate([pairs[0], seat]).astype(jnp.int32), live_count, need, row_p, weights, done_rows, ours, others, trailing
+    )
     return lower_first, lower_second, owned
 
 

time: 270 us -> 255 us (0.944)
  the two profiles are of different devices: /device:TPU:0 before, /device:TPU:58 now
where the time goes in v1:
time: 255 us; the launch traced here: 253 us
  Pallas kernels  183 us (72%)
  waiting for transfers between devices  29.5 us (12%)
  starting transfers between devices  15.1 us (6%)
  between operations  14.8 us (6%)
  local copies, waits for them, and re-layouts  7.62 us (3%)
  other arithmetic  2.87 us (1%)
    pallas_call x1, Pallas kernels, second_stage(): pl.pallas_call(second_kernel, out_shape=[jax.ShapeDtypeStruct((N, N), BF1...  57.3 us
    pallas_call x1, Pallas kernels, final_stage(): pl.pallas_call(final_kernel, out_shape=jax.ShapeDtypeStruct(trailing.shap...  39.8 us
    pallas_call x1, Pallas kernels, first_stage(): pl.pallas_call(first_kernel, out_shape=[jax.ShapeDtypeStruct((N, N), BF16...  39.8 us
    pallas_call x1, Pallas kernels, rows_stage(): pl.pallas_call(rows_kernel, out_shape=jax.ShapeDtypeStruct((count, HALF,...  27.7 us
    pallas_call x1, Pallas kernels, cols_stage(): pl.pallas_call(cols_kernel, out_shape=[jax.ShapeDtypeStruct((1, HALF, N),...  18.2 us
    ppermute x1, waiting for transfers between devices, spread(): up = lax.ppermute(unit, 'row', [(r, (r + 2) % nrow) for r in range(nrow)])  11.2 us
    ppermute x1, waiting for transfers between devices, spread(): lax.ppermute(jnp.where(core == 0, up, down), 'row', [(r, (r + (2 if r % 2...  7.44 us
    ppermute x2, waiting for transfers between devices, spread(): lax.ppermute(x, ('row', 'col'), [(flat(r, c + r + off), flat(r, c)) for r...  6.88 us
  transfers between devices with their start and end apart: 12, of which 4 were waited for; matrix products, arithmetic and copies ran while one was open for 3% of the time, Pallas kernels for 57%

profile of v1, /device:TPU:58, one launch (start us, length us, event | category | flops | bytes accessed | tf_op | source)
XLA Modules:
  0.0 252.7 jit_solution(2797360236803354946)
XLA Ops:
  7.2 0.7 all-gather.4.cloned.1.call-update
  8.0 1.1 constant_dynamic-update-slice_fusion.1
  9.0 1.1 constant_dynamic-update-slice_fusion.a0
  10.1 1.0 copy-done
  11.2 1.9 collective-permute-start.1
  13.1 3.6 %collective-permute-start = (bf16[128,1024]{1,0:T(8,128)(2,1)S(1)}, bf16[128,1024]{1,0:T(8,128)(2,1)S(1)}, u32[]{:S(2)}, u32[]{:S(2)}) collective-permute-start(bf16[128,1024]{1,0:T(8,128)(2,1)S(1)} %constant_dynamic-update-slice_fusion.2), channel_id=1, source_target_pairs={{0,0},{1,1},{2,2},{3,3},{4,4},{5,5},{6,6},{7,7},{8,8},{9,9},{10,10... | collective-permute-start | bytes 786440 | tf_op jit(solution)/shard_map/ppermute | solution.py:430
  16.7 6.9 %collective-permute-done.1 = bf16[128,1024]{1,0:T(8,128)(2,1)S(1)} collective-permute-done((bf16[128,1024]{1,0:T(8,128)(2,1)S(1)}, bf16[128,1024]{1,0:T(8,128)(2,1)S(1)}, u32[]{:S(2)}, u32[]{:S(2)}) %collective-permute-start.1) | collective-permute-done | bytes 262176 | tf_op jit(solution)/shard_map/ppermute | solution.py:430
  23.6 2.0 collective-permute-start.3
  25.6 0.1 collective-permute-start.2
  25.7 0.7 constant_dynamic-update-slice_fusion.8
  26.4 0.7 constant_dynamic-update-slice_fusion.7
  27.1 11.2 %collective-permute-done.3 = bf16[2,128,1024]{2,1,0:T(8,128)(2,1)S(1)} collective-permute-done((bf16[2,128,1024]{2,1,0:T(8,128)(2,1)S(1)}, bf16[2,128,1024]{2,1,0:T(8,128)(2,1)S(1)}, u32[]{:S(2)}, u32[]{:S(2)}) %collective-permute-start.3) | collective-permute-done | bytes 524320 | tf_op jit(solution)/shard_map/ppermute | solution.py:434
  38.4 3.3 %collective-permute-done.2 = bf16[2,128,1024]{2,1,0:T(8,128)(2,1)S(1)} collective-permute-done((bf16[2,128,1024]{2,1,0:T(8,128)(2,1)S(1)}, bf16[2,128,1024]{2,1,0:T(8,128)(2,1)S(1)}, u32[]{:S(2)}, u32[]{:S(2)}) %collective-permute-start.2) | collective-permute-done | bytes 524320 | tf_op jit(solution)/shard_map/ppermute | solution.py:435
  41.7 1.0 broadcast_select_fusion
  42.7 1.7 collective-permute-start.4
  44.4 7.4 %collective-permute-done.4 = bf16[2,128,1024]{2,1,0:T(8,128)(2,1)S(1)} collective-permute-done((bf16[2,128,1024]{2,1,0:T(8,128)(2,1)S(1)}, bf16[2,128,1024]{2,1,0:T(8,128)(2,1)S(1)}, u32[]{:S(2)}, u32[]{:S(2)}) %collective-permute-start.4) | collective-permute-done | bytes 524320 | tf_op jit(solution)/shard_map/ppermute | solution.py:438
  51.9 0.8 constant_dynamic-update-slice_fusion.5
  52.7 0.8 constant_dynamic-update-slice_fusion.4.mine
  53.5 0.5 fusion.4.where
  54.1 1.7 collective-permute-start.7
  55.8 2.4 collective-permute-start.6
  58.2 1.2 collective-permute-start.5
  59.5 39.8 %first_stage.1 = (bf16[1024,1024]{1,0:T(8,128)(2,1)}, bf16[1024,1024]{1,0:T(8,128)(2,1)}) custom-call(bf16[1024,1024]{1,0:T(8,128)(2,1)} %all-gather.4.cloned.1.call-done.g_ref), custom_call_target="tpu_custom_call" | custom-call | flops 10000000000 | bytes 10000000 | tf_op jit(solution)/shard_map/first_stage/pallas_call | solution.py:222
  99.2 1.3 copy-done.5
  100.6 57.3 %second_stage.1 = (bf16[1024,1024]{1,0:T(8,128)(2,1)}, bf16[1024,1024]{1,0:T(8,128)(2,1)}, bf16[1024,1024]{1,0:T(8,128)(2,1)}, bf16[1024,1024]{1,0:T(8,128)(2,1)}) custom-call(s32[16]{0:T(128)} %fusion.4.where, bf16[8,128,1024]{2,1,0:T(8,128)(2,1)} %constant_dynamic-update-slice_fusion.4.mine, bf16[8,128,1024]{2,1,0:T(8,128)(2,1)} %copy-done.5, ...), custom_call_target="tpu_custom_call" | custom-call | flops 20000000000 | bytes 10000000 | tf_op jit(solution)/shard_map/second_stage/pallas_call | solution.py:235
  157.9 18.2 %cols_stage.1 = (bf16[1,256,1024]{2,1,0:T(8,128)(2,1)}, bf16[1,256,1024]{2,1,0:T(8,128)(2,1)}, bf16[4,256,2048]{2,1,0:T(8,128)(2,1)}) custom-call(bf16[2,256,1024]{2,1,0:T(8,128)(2,1)} %copy-done, bf16[2,256,1024]{2,1,0:T(8,128)(2,1)} %collective-permute-done.5.a1, bf16[2,256,1024]{2,1,0:T(8,128)(2,1)} %collective-permute-done.6.a2, ...), custom_call_target="tpu_custom_call" | custom-call | flops 10000000000 | bytes 30000000 | tf_op jit(solution)/shard_map/cols_stage/pallas_call | solution.py:311
  176.1 0.3 collective-permute-start.9
  177.1 0.1 fusion.1
  177.2 0.5 convert_element_type.2.need
  177.8 0.6 pad_add_fusion.pairs
  178.3 27.7 %rows_stage.1.done_rows = bf16[8,256,2048]{2,1,0:T(8,128)(2,1)} custom-call(s32[8]{0:T(128)} %convert_element_type.2.need, bf16[16,2,256,1024]{3,2,1,0:T(8,128)(2,1)} %bitcast.26, bf16[1024,1024]{1,0:T(8,128)(2,1)} %get-tuple-element.15.w1h, bf16[1024,1024]{1,0:T(8,128)(2,1)} %get-tuple-element.16.w1l, bf16[1024,1024]{1,0:T(8,128)(2,1)} %get-tuple-element.18.w2h, ...), custom_call_target="tpu_custom_call" | custom-call | flops 20000000000 | bytes 40000000 | tf_op jit(solution)/shard_map/rows_stage/pallas_call | solution.py:336
  206.1 39.8 %final_stage.1 = f32[1,24,256,256]{3,2,1,0:T(8,128)} custom-call(s32[48]{0:T(128)} %pad_add_fusion.pairs, s32[1]{0:T(128)} %copy.17.live, s32[8]{0:T(128)} %convert_element_type.2.need, bf16[16,2,256,1024]{3,2,1,0:T(8,128)(2,1)} %bitcast.27, bf16[1024,1024]{1,0:T(8,128)(2,1)} %get-tuple-element.15.w1h, bf16[1024,1024]{1,0:T(8,128)(2,1)} %get-tuple-element.16.w1l, ...), custom_call_target="tpu_custom_call" | custom-call | flops 30000001024 | bytes 40000000 | tf_op jit(solution)/shard_map/final_stage/pallas_call | solution.py:402
  (28 shorter events, 0.2 us)
Async XLA Ops:
  7.2 4.0 %copy-start.2 = (bf16[64,1024]{1,0:T(8,128)(2,1)S(1)}, bf16[64,1024]{1,0:T(8,128)(2,1)}, u32[]{:S(2)}) copy-start(bf16[64,1024]{1,0:T(8,128)(2,1)} %param.11) | copy-start | bytes 393220
  7.2 4.0 %copy-start.3 = (bf16[64,1024]{1,0:T(8,128)(2,1)S(1)}, bf16[64,1024]{1,0:T(8,128)(2,1)}, u32[]{:S(2)}) copy-start(bf16[64,1024]{1,0:T(8,128)(2,1)} %param.12) | copy-start | bytes 393220
  7.2 52.3 %all-gather.4.cloned.1.call-start = ((), (), s32[]{:S(2)}) async-start(), calls=%async_computation | async-start | bytes 2228224 | tf_op jit(solution)/shard_map/all_gather | solution.py:453
  7.9 170.4 %all-gather.6.cloned.1.call-start = ((), (), s32[]{:S(2)}) async-start(), calls=%async_computation.1 | async-start | bytes 17825792 | tf_op jit(solution)/shard_map/all_gather | solution.py:456
  10.1 1.0 copy-start
  11.2 12.3 %collective-permute-start.1 = (bf16[128,1024]{1,0:T(8,128)(2,1)S(1)}, bf16[128,1024]{1,0:T(8,128)(2,1)S(1)}, u32[]{:S(2)}, u32[]{:S(2)}) collective-permute-start(bf16[128,1024]{1,0:T(8,128)(2,1)S(1)} %constant_dynamic-update-slice_fusion.2), channel_id=1, source_target_pairs={{8,0},{9,1},{10,2},{11,3},{12,4},{13,5},{14,6},{15,7},{0,8},{1,9},... | collective-permute-start | bytes 786440 | tf_op jit(solution)/shard_map/ppermute | solution.py:430
  13.1 10.5 %collective-permute-start = (bf16[128,1024]{1,0:T(8,128)(2,1)S(1)}, bf16[128,1024]{1,0:T(8,128)(2,1)S(1)}, u32[]{:S(2)}, u32[]{:S(2)}) collective-permute-start(bf16[128,1024]{1,0:T(8,128)(2,1)S(1)} %constant_dynamic-update-slice_fusion.2), channel_id=1, source_target_pairs={{0,0},{1,1},{2,2},{3,3},{4,4},{5,5},{6,6},{7,7},{8,8},{9,9},{10,10... | collective-permute-start | bytes 786440 | tf_op jit(solution)/shard_map/ppermute | solution.py:430
  23.6 14.8 %collective-permute-start.3 = (bf16[2,128,1024]{2,1,0:T(8,128)(2,1)S(1)}, bf16[2,128,1024]{2,1,0:T(8,128)(2,1)S(1)}, u32[]{:S(2)}, u32[]{:S(2)}) collective-permute-start(bf16[2,128,1024]{2,1,0:T(8,128)(2,1)S(1)} %pad_maximum_fusion), channel_id=1, source_target_pairs={{0,32},{16,48},{32,64},{48,80},{64,96},{80,112},{96,0},{112,16},{1... | collective-permute-start | bytes 1572872 | tf_op jit(solution)/shard_map/ppermute | solution.py:434
  25.6 16.1 %collective-permute-start.2 = (bf16[2,128,1024]{2,1,0:T(8,128)(2,1)S(1)}, bf16[2,128,1024]{2,1,0:T(8,128)(2,1)S(1)}, u32[]{:S(2)}, u32[]{:S(2)}) collective-permute-start(bf16[2,128,1024]{2,1,0:T(8,128)(2,1)S(1)} %pad_maximum_fusion), channel_id=1, source_target_pairs={{0,96},{16,112},{32,0},{48,16},{64,32},{80,48},{96,64},{112,80},{1... | collective-permute-start | bytes 1572872 | tf_op jit(solution)/shard_map/ppermute | solution.py:435
  27.1 26.9 %copy-start.1 = (bf16[2,256,1024]{2,1,0:T(8,128)(2,1)S(1)}, bf16[2,256,1024]{2,1,0:T(8,128)(2,1)}, u32[]{:S(2)}) copy-start(bf16[2,256,1024]{2,1,0:T(8,128)(2,1)} %copy-done) | copy-start | bytes 3145732
  42.7 9.2 %collective-permute-start.4 = (bf16[2,128,1024]{2,1,0:T(8,128)(2,1)S(1)}, bf16[2,128,1024]{2,1,0:T(8,128)(2,1)S(1)}, u32[]{:S(2)}, u32[]{:S(2)}) collective-permute-start(bf16[2,128,1024]{2,1,0:T(8,128)(2,1)S(1)} %get-tuple-element.25), channel_id=1, source_target_pairs={{0,32},{16,112},{32,64},{48,16},{64,96},{80,48},{96,0},{112,80},{1... | collective-permute-start | bytes 1572872 | tf_op jit(solution)/shard_map/ppermute | solution.py:438
  53.5 45.7 %collective-permute-start.8 = (bf16[8,128,1024]{2,1,0:T(8,128)(2,1)}, bf16[8,128,1024]{2,1,0:T(8,128)(2,1)S(1)}, u32[]{:S(2)}, u32[]{:S(2)}) collective-permute-start(bf16[8,128,1024]{2,1,0:T(8,128)(2,1)} %constant_dynamic-update-slice_fusion.4.mine), channel_id=1, source_target_pairs={{0,16},{16,0},{32,48},{48,32},{64,80},{80,64},{96,112},{112,96},{1... | collective-permute-start | bytes 6291464 | tf_op jit(solution)/shard_map/ppermute | solution.py:442
  54.1 103.8 %collective-permute-start.7 = (bf16[2,256,1024]{2,1,0:T(8,128)(2,1)S(1)}, bf16[2,256,1024]{2,1,0:T(8,128)(2,1)}, u32[]{:S(2)}, u32[]{:S(2)}) collective-permute-start(bf16[2,256,1024]{2,1,0:T(8,128)(2,1)S(1)} %copy-done.1), channel_id=1, source_target_pairs={{0,32},{16,48},{32,64},{48,80},{64,96},{80,112},{96,0},{112,16},{1... | collective-permute-start | bytes 3145736 | tf_op jit(solution)/shard_map/ppermute | solution.py:459
  55.8 102.0 %collective-permute-start.6 = (bf16[2,256,1024]{2,1,0:T(8,128)(2,1)S(1)}, bf16[2,256,1024]{2,1,0:T(8,128)(2,1)}, u32[]{:S(2)}, u32[]{:S(2)}) collective-permute-start(bf16[2,256,1024]{2,1,0:T(8,128)(2,1)S(1)} %copy-done.1), channel_id=1, source_target_pairs={{0,64},{16,80},{32,96},{48,112},{64,0},{80,16},{96,32},{112,48},{1... | collective-permute-start | bytes 3145736 | tf_op jit(solution)/shard_map/ppermute | solution.py:459
  58.2 99.6 %collective-permute-start.5 = (bf16[2,256,1024]{2,1,0:T(8,128)(2,1)S(1)}, bf16[2,256,1024]{2,1,0:T(8,128)(2,1)}, u32[]{:S(2)}, u32[]{:S(2)}) collective-permute-start(bf16[2,256,1024]{2,1,0:T(8,128)(2,1)S(1)} %copy-done.1), channel_id=1, source_target_pairs={{0,96},{16,112},{32,0},{48,16},{64,32},{80,48},{96,64},{112,80},{1... | collective-permute-start | bytes 3145736 | tf_op jit(solution)/shard_map/ppermute | solution.py:459
  99.2 1.3 copy-start.5
  157.9 19.2 %copy-start.4 = (s32[1,2,24]{2,1,0:T(2,128)S(1)}, s32[1,2,24]{2,1,0:T(2,128)}, u32[]{:S(2)}) copy-start(s32[1,2,24]{2,1,0:T(2,128)} %param.14) | copy-start | bytes 580
  176.1 29.9 %collective-permute-start.9 = (bf16[4,256,2048]{2,1,0:T(8,128)(2,1)}, bf16[4,256,2048]{2,1,0:T(8,128)(2,1)}, u32[]{:S(2)}, u32[]{:S(2)}) collective-permute-start(bf16[4,256,2048]{2,1,0:T(8,128)(2,1)} %get-tuple-element.24.mine), channel_id=1, source_target_pairs={{0,16},{16,0},{32,48},{48,32},{64,80},{80,64},{96,112},{112,96},{1... | collective-permute-start | bytes 12582920 | tf_op jit(solution)/shard_map/ppermute | solution.py:470
Sparse Core Ops, SparseCore 0:
  10.1 47.2 all-gather.3
  59.6 110.7 all-gather.5

commit v2 on v1

--- a/solution.py
+++ b/solution.py
@@ -99,9 +99,16 @@
             z1 = apply(assemble(lambda i, k: v1[k, i] if i <= k else None), w1r)
             z1r = spread_rows(z1)
             y = w0 - apply(assemble(lambda i, k: qs[i][k]), z1r)
-            zr = spread_rows(apply(v0t, spread_rows(y))) + z1r
+            z0 = apply(v0t, spread_rows(y))
+            zr = spread_rows(z0) + z1r
             both = in0 | in1
-            for t in range(s + 2, count):
+            if s + 4 < count:
+                lhs = jnp.concatenate([b0, b1], axis=0)[:, Q * (s + 4) :]
+                rhs = jnp.concatenate([z0, z1], axis=0)
+                away = lax.dot_general(lhs, rhs, (((0,), (0,)), ((), ())), precision=lax.Precision.HIGHEST, preferred_element_type=F32)
+                for t in range(s + 4, count):
+                    tiles[t] = jnp.where(both, 0.0, tiles[t]) - away[Q * (t - s - 4) : Q * (t - s - 3), :]
+            for t in range(s + 2, min(s + 4, count)):
                 row = tiles[t]
                 terms = [lanes(row, c0 + m) * zr[m] for m in range(2 * Q)]
                 tiles[t] = jnp.where(both, 0.0, row) - total(terms)
@@ -126,7 +133,8 @@
             rows = pl.ds(pl.multiple_of(p * 2 * NB, 2 * NB), 2 * NB)
             ah, al = rh[rows, cols], rl[rows, cols]
             bh, bl = rh[rows, :], rl[rows, :]
-            tri[...] -= dot(ah, bh, K0) + dot(ah, bl, K0) + dot(al, bh, K0)
+            pair = dot(jnp.concatenate([ah, al], axis=1), bh, K0)
+            tri[...] -= pair[0:NB] + pair[NB:] + dot(ah, bl, K0)
             return c
 
         lax.fori_loop(0, (k + 1) // 2, update, 0)
@@ -138,7 +146,8 @@
         tri[:, pl.ds(k0, NB)] = jnp.eye(NB, dtype=F32)
         wh, wl = split(w)
         xh, xl = split(tri[...])
-        row = dot(wh, xh, KM) + dot(wh, xl, KM) + dot(wl, xh, KM)
+        pair = dot(jnp.concatenate([wh, wl], axis=0), xh, KM)
+        row = pair[0:NB] + pair[NB:] + dot(wh, xl, KM)
         oh, ol = split(row)
         rh[pl.ds(k0, NB), :] = oh
         rl[pl.ds(k0, NB), :] = ol
@@ -187,7 +196,8 @@
 
         def inner(j, c):
             t = pl.ds(pl.multiple_of(j * half, half), half)
-            prod = dot(ch[s, :], ch[t, :], KT) + dot(ch[s, :], cl[t, :], KT) + dot(cl[s, :], ch[t, :], KT)
+            pair = dot(jnp.concatenate([ch[s, :], cl[s, :]], axis=0), ch[t, :], KT)
+            prod = pair[0:half] + pair[half:] + dot(ch[s, :], cl[t, :], KT)
             shifted[s, t] = diag[s, t].astype(F32) - prod
             return c
 
@@ -464,13 +474,15 @@
     active = jnp.arange(pairs.shape[1], dtype=jnp.int32) < live_count[0]
     group = jnp.arange(ncol // PER, dtype=jnp.int32)
     need = jnp.any((pairs[0][None] // PER == group[:, None]) & active[None], axis=1).astype(jnp.int32)
+    seats = jnp.concatenate([pairs[0], seat]).astype(jnp.int32)
+    whole_first, where, need, seats = lax.optimization_barrier((whole_first, where, need, seats))
     w1h, w1l = first_stage(whole_first)
     weights = (w1h, w1l, *second_stage(where, mine, theirs, w1h, w1l))
     lower_first, lower_second, ours = cols_stage((held, down, far, up), weights)
     others = lax.ppermute(ours, "row", [(r, r ^ 1) for r in range(nrow)])
     done_rows = rows_stage(need, row_p, weights)
     owned = final_stage(
-        jnp.concatenate([pairs[0], seat]).astype(jnp.int32), live_count, need, row_p, weights, done_rows, ours, others, trailing
+        seats, live_count, need, row_p, weights, done_rows, ours, others, trailing
     )
     return lower_first, lower_second, owned
 

time: 255 us -> 250 us (0.980)
  the two profiles are of different devices: /device:TPU:58 before, /device:TPU:16 now
where the time goes in v2:
time: 250 us; the launch traced here: 248 us
  Pallas kernels  177 us (71%)
  waiting for transfers between devices  26.6 us (11%)
  starting transfers between devices  18.9 us (8%)
  between operations  14.9 us (6%)
  local copies, waits for them, and re-layouts  7.57 us (3%)
  other arithmetic  2.98 us (1%)
    pallas_call x1, Pallas kernels, second_stage(): pl.pallas_call(second_kernel, out_shape=[jax.ShapeDtypeStruct((N, N), BF1...  54.7 us
    pallas_call x1, Pallas kernels, final_stage(): pl.pallas_call(final_kernel, out_shape=jax.ShapeDtypeStruct(trailing.shap...  39.8 us
    pallas_call x1, Pallas kernels, first_stage(): pl.pallas_call(first_kernel, out_shape=[jax.ShapeDtypeStruct((N, N), BF16...  37.1 us
    pallas_call x1, Pallas kernels, rows_stage(): pl.pallas_call(rows_kernel, out_shape=jax.ShapeDtypeStruct((count, HALF,...  27.7 us
    pallas_call x1, Pallas kernels, cols_stage(): pl.pallas_call(cols_kernel, out_shape=[jax.ShapeDtypeStruct((1, HALF, N),...  18.2 us
    ppermute x2, waiting for transfers between devices, spread(): lax.ppermute(x, ('row', 'col'), [(flat(r, c + r + off), flat(r, c)) for r...  9.55 us
    ppermute x1, waiting for transfers between devices, spread(): lax.ppermute(jnp.where(core == 0, up, down), 'row', [(r, (r + (2 if r % 2...  8.86 us
    ppermute x1, starting transfers between devices, spread(): up = lax.ppermute(unit, 'row', [(r, (r + 2) % nrow) for r in range(nrow)])  8.42 us
  transfers between devices with their start and end apart: 12, of which 3 were waited for; matrix products, arithmetic and copies ran while one was open for 3% of the time, Pallas kernels for 55%

profile of v2, /device:TPU:16, one launch (start us, length us, event | category | flops | bytes accessed | tf_op | source)
XLA Modules:
  0.0 248.3 jit_solution(5247678115350180289)
XLA Ops:
  7.2 0.7 all-gather.4.cloned.1.call-update
  8.0 1.1 constant_dynamic-update-slice_fusion.1
  9.0 1.1 constant_dynamic-update-slice_fusion.a0
  10.1 1.0 copy-done
  11.2 0.3 collective-permute-start.1
  11.5 0.7 collective-permute-start
  12.2 9.5 %collective-permute-done.1 = bf16[128,1024]{1,0:T(8,128)(2,1)S(1)} collective-permute-done((bf16[128,1024]{1,0:T(8,128)(2,1)S(1)}, bf16[128,1024]{1,0:T(8,128)(2,1)S(1)}, u32[]{:S(2)}, u32[]{:S(2)}) %collective-permute-start.1) | collective-permute-done | bytes 262176 | tf_op jit(solution)/shard_map/ppermute | solution.py:440
  21.8 8.4 %collective-permute-start.3 = (bf16[2,128,1024]{2,1,0:T(8,128)(2,1)S(1)}, bf16[2,128,1024]{2,1,0:T(8,128)(2,1)S(1)}, u32[]{:S(2)}, u32[]{:S(2)}) collective-permute-start(bf16[2,128,1024]{2,1,0:T(8,128)(2,1)S(1)} %pad_maximum_fusion), channel_id=1, source_target_pairs={{0,32},{16,48},{32,64},{48,80},{64,96},{80,112},{96,0},{112,16},{1... | collective-permute-start | bytes 1572872 | tf_op jit(solution)/shard_map/ppermute | solution.py:444
  30.2 2.7 %collective-permute-start.2 = (bf16[2,128,1024]{2,1,0:T(8,128)(2,1)S(1)}, bf16[2,128,1024]{2,1,0:T(8,128)(2,1)S(1)}, u32[]{:S(2)}, u32[]{:S(2)}) collective-permute-start(bf16[2,128,1024]{2,1,0:T(8,128)(2,1)S(1)} %pad_maximum_fusion), channel_id=1, source_target_pairs={{0,96},{16,112},{32,0},{48,16},{64,32},{80,48},{96,64},{112,80},{1... | collective-permute-start | bytes 1572872 | tf_op jit(solution)/shard_map/ppermute | solution.py:445
  32.9 0.7 constant_dynamic-update-slice_fusion.8
  33.6 0.7 constant_dynamic-update-slice_fusion.7
  34.3 7.4 %collective-permute-done.3 = bf16[2,128,1024]{2,1,0:T(8,128)(2,1)S(1)} collective-permute-done((bf16[2,128,1024]{2,1,0:T(8,128)(2,1)S(1)}, bf16[2,128,1024]{2,1,0:T(8,128)(2,1)S(1)}, u32[]{:S(2)}, u32[]{:S(2)}) %collective-permute-start.3) | collective-permute-done | bytes 524320 | tf_op jit(solution)/shard_map/ppermute | solution.py:444
  41.8 1.0 broadcast_select_fusion
  42.8 1.5 collective-permute-start.4
  44.3 8.9 %collective-permute-done.4 = bf16[2,128,1024]{2,1,0:T(8,128)(2,1)S(1)} collective-permute-done((bf16[2,128,1024]{2,1,0:T(8,128)(2,1)S(1)}, bf16[2,128,1024]{2,1,0:T(8,128)(2,1)S(1)}, u32[]{:S(2)}, u32[]{:S(2)}) %collective-permute-start.4) | collective-permute-done | bytes 524320 | tf_op jit(solution)/shard_map/ppermute | solution.py:448
  53.2 0.8 constant_dynamic-update-slice_fusion.5
  54.0 0.8 constant_dynamic-update-slice_fusion.4.mine
  55.5 0.1 fusion.1
  55.6 0.6 convert_element_type.2.need
  56.2 0.5 fusion.4.where
  56.8 0.7 pad_add_fusion.pairs
  57.4 0.3 collective-permute-start.7
  57.8 3.0 %collective-permute-start.6 = (bf16[2,256,1024]{2,1,0:T(8,128)(2,1)S(1)}, bf16[2,256,1024]{2,1,0:T(8,128)(2,1)S(1)}, u32[]{:S(2)}, u32[]{:S(2)}) collective-permute-start(bf16[2,256,1024]{2,1,0:T(8,128)(2,1)S(1)} %copy-done.1), channel_id=1, source_target_pairs={{0,64},{16,80},{32,96},{48,112},{64,0},{80,16},{96,32},{112,48},{1... | collective-permute-start | bytes 3145736 | tf_op jit(solution)/shard_map/ppermute | solution.py:469
  60.7 1.6 collective-permute-start.5
  62.3 37.1 %first_stage.1 = (bf16[1024,1024]{1,0:T(8,128)(2,1)}, bf16[1024,1024]{1,0:T(8,128)(2,1)}) custom-call(bf16[1024,1024]{1,0:T(8,128)(2,1)} %all-gather.4.cloned.1.call-done.g_ref), custom_call_target="tpu_custom_call" | custom-call | flops 10000000000 | bytes 10000000 | tf_op jit(solution)/shard_map/first_stage/pallas_call | solution.py:232
  99.4 54.7 %second_stage.1 = (bf16[1024,1024]{1,0:T(8,128)(2,1)}, bf16[1024,1024]{1,0:T(8,128)(2,1)}, bf16[1024,1024]{1,0:T(8,128)(2,1)}, bf16[1024,1024]{1,0:T(8,128)(2,1)}) custom-call(s32[16]{0:T(128)} %fusion.4.where, bf16[8,128,1024]{2,1,0:T(8,128)(2,1)} %constant_dynamic-update-slice_fusion.4.mine, bf16[8,128,1024]{2,1,0:T(8,128)(2,1)} %collective-permute-done.8.theirs, ...), custom_call_target="tpu_custom_call" | custom-call | flops 20000000000 | bytes 10000000 | tf_op jit(solution)/shard_map/second_stage/pallas_call | solution.py:245
  154.1 0.9 copy-done.5
  155.1 0.3 copy-done.6
  155.4 18.2 %cols_stage.1 = (bf16[1,256,1024]{2,1,0:T(8,128)(2,1)}, bf16[1,256,1024]{2,1,0:T(8,128)(2,1)}, bf16[4,256,2048]{2,1,0:T(8,128)(2,1)}) custom-call(bf16[2,256,1024]{2,1,0:T(8,128)(2,1)} %copy-done, bf16[2,256,1024]{2,1,0:T(8,128)(2,1)} %collective-permute-done.5.a1, bf16[2,256,1024]{2,1,0:T(8,128)(2,1)} %copy-done.6, bf16[2,256,1024]{2,1,0:T(8,128)(2,1)} %copy-done.5, ...), custom_call_target="tpu_custom_call" | custom-call | flops 10000000000 | bytes 30000000 | tf_op jit(solution)/shard_map/cols_stage/pallas_call | solution.py:321
  173.6 0.3 collective-permute-start.9
  173.9 27.7 %rows_stage.1.done_rows = bf16[8,256,2048]{2,1,0:T(8,128)(2,1)} custom-call(s32[8]{0:T(128)} %convert_element_type.2.need, bf16[16,2,256,1024]{3,2,1,0:T(8,128)(2,1)} %bitcast.26, bf16[1024,1024]{1,0:T(8,128)(2,1)} %get-tuple-element.20.w1h, bf16[1024,1024]{1,0:T(8,128)(2,1)} %get-tuple-element.21.w1l, bf16[1024,1024]{1,0:T(8,128)(2,1)} %get-tuple-element.24.w2h, ...), custom_call_target="tpu_custom_call" | custom-call | flops 20000000000 | bytes 40000000 | tf_op jit(solution)/shard_map/rows_stage/pallas_call | solution.py:346
  201.7 39.8 %final_stage.1 = f32[1,24,256,256]{3,2,1,0:T(8,128)} custom-call(s32[48]{0:T(128)} %pad_add_fusion.pairs, s32[1]{0:T(128)} %copy.17.live, s32[8]{0:T(128)} %convert_element_type.2.need, bf16[16,2,256,1024]{3,2,1,0:T(8,128)(2,1)} %bitcast.27, bf16[1024,1024]{1,0:T(8,128)(2,1)} %get-tuple-element.20.w1h, bf16[1024,1024]{1,0:T(8,128)(2,1)} %get-tuple-element.21.w1l, ...), custom_call_target="tpu_custom_call" | custom-call | flops 30000001024 | bytes 40000000 | tf_op jit(solution)/shard_map/final_stage/pallas_call | solution.py:412
  (30 shorter events, 0.3 us)
Async XLA Ops:
  7.2 4.0 %copy-start.2 = (bf16[64,1024]{1,0:T(8,128)(2,1)S(1)}, bf16[64,1024]{1,0:T(8,128)(2,1)}, u32[]{:S(2)}) copy-start(bf16[64,1024]{1,0:T(8,128)(2,1)} %param.11) | copy-start | bytes 393220
  7.2 4.0 %copy-start.3 = (bf16[64,1024]{1,0:T(8,128)(2,1)S(1)}, bf16[64,1024]{1,0:T(8,128)(2,1)}, u32[]{:S(2)}) copy-start(bf16[64,1024]{1,0:T(8,128)(2,1)} %param.12) | copy-start | bytes 393220
  7.2 55.2 %all-gather.4.cloned.1.call-start = ((), (), s32[]{:S(2)}) async-start(), calls=%async_computation | async-start | bytes 2228224 | tf_op jit(solution)/shard_map/all_gather | solution.py:463
  7.9 166.0 %all-gather.6.cloned.1.call-start = ((), (), s32[]{:S(2)}) async-start(), calls=%async_computation.1 | async-start | bytes 17825792 | tf_op jit(solution)/shard_map/all_gather | solution.py:466
  10.1 1.0 copy-start
  11.2 10.5 %collective-permute-start.1 = (bf16[128,1024]{1,0:T(8,128)(2,1)S(1)}, bf16[128,1024]{1,0:T(8,128)(2,1)S(1)}, u32[]{:S(2)}, u32[]{:S(2)}) collective-permute-start(bf16[128,1024]{1,0:T(8,128)(2,1)S(1)} %constant_dynamic-update-slice_fusion.2), channel_id=1, source_target_pairs={{8,0},{9,1},{10,2},{11,3},{12,4},{13,5},{14,6},{15,7},{0,8},{1,9},... | collective-permute-start | bytes 786440 | tf_op jit(solution)/shard_map/ppermute | solution.py:440
  11.5 10.2 %collective-permute-start = (bf16[128,1024]{1,0:T(8,128)(2,1)S(1)}, bf16[128,1024]{1,0:T(8,128)(2,1)S(1)}, u32[]{:S(2)}, u32[]{:S(2)}) collective-permute-start(bf16[128,1024]{1,0:T(8,128)(2,1)S(1)} %constant_dynamic-update-slice_fusion.2), channel_id=1, source_target_pairs={{0,0},{1,1},{2,2},{3,3},{4,4},{5,5},{6,6},{7,7},{8,8},{9,9},{10,10... | collective-permute-start | bytes 786440 | tf_op jit(solution)/shard_map/ppermute | solution.py:440
  21.8 20.0 %collective-permute-start.3 = (bf16[2,128,1024]{2,1,0:T(8,128)(2,1)S(1)}, bf16[2,128,1024]{2,1,0:T(8,128)(2,1)S(1)}, u32[]{:S(2)}, u32[]{:S(2)}) collective-permute-start(bf16[2,128,1024]{2,1,0:T(8,128)(2,1)S(1)} %pad_maximum_fusion), channel_id=1, source_target_pairs={{0,32},{16,48},{32,64},{48,80},{64,96},{80,112},{96,0},{112,16},{1... | collective-permute-start | bytes 1572872 | tf_op jit(solution)/shard_map/ppermute | solution.py:444
  30.2 11.6 %collective-permute-start.2 = (bf16[2,128,1024]{2,1,0:T(8,128)(2,1)S(1)}, bf16[2,128,1024]{2,1,0:T(8,128)(2,1)S(1)}, u32[]{:S(2)}, u32[]{:S(2)}) collective-permute-start(bf16[2,128,1024]{2,1,0:T(8,128)(2,1)S(1)} %pad_maximum_fusion), channel_id=1, source_target_pairs={{0,96},{16,112},{32,0},{48,16},{64,32},{80,48},{96,64},{112,80},{1... | collective-permute-start | bytes 1572872 | tf_op jit(solution)/shard_map/ppermute | solution.py:445
  34.3 21.2 %copy-start.4 = (s32[1,2,24]{2,1,0:T(2,128)S(1)}, s32[1,2,24]{2,1,0:T(2,128)}, u32[]{:S(2)}) copy-start(s32[1,2,24]{2,1,0:T(2,128)} %param.14) | copy-start | bytes 580
  34.3 23.1 %copy-start.1 = (bf16[2,256,1024]{2,1,0:T(8,128)(2,1)S(1)}, bf16[2,256,1024]{2,1,0:T(8,128)(2,1)}, u32[]{:S(2)}) copy-start(bf16[2,256,1024]{2,1,0:T(8,128)(2,1)} %copy-done) | copy-start | bytes 3145732
  42.8 10.4 %collective-permute-start.4 = (bf16[2,128,1024]{2,1,0:T(8,128)(2,1)S(1)}, bf16[2,128,1024]{2,1,0:T(8,128)(2,1)S(1)}, u32[]{:S(2)}, u32[]{:S(2)}) collective-permute-start(bf16[2,128,1024]{2,1,0:T(8,128)(2,1)S(1)} %get-tuple-element.33), channel_id=1, source_target_pairs={{0,32},{16,112},{32,64},{48,16},{64,96},{80,48},{96,0},{112,80},{1... | collective-permute-start | bytes 1572872 | tf_op jit(solution)/shard_map/ppermute | solution.py:448
  54.8 44.6 %collective-permute-start.8 = (bf16[8,128,1024]{2,1,0:T(8,128)(2,1)}, bf16[8,128,1024]{2,1,0:T(8,128)(2,1)}, u32[]{:S(2)}, u32[]{:S(2)}) collective-permute-start(bf16[8,128,1024]{2,1,0:T(8,128)(2,1)} %constant_dynamic-update-slice_fusion.4.mine), channel_id=1, source_target_pairs={{0,16},{16,0},{32,48},{48,32},{64,80},{80,64},{96,112},{112,96},{1... | collective-permute-start | bytes 6291464 | tf_op jit(solution)/shard_map/ppermute | solution.py:452
  57.4 96.7 %collective-permute-start.7 = (bf16[2,256,1024]{2,1,0:T(8,128)(2,1)S(1)}, bf16[2,256,1024]{2,1,0:T(8,128)(2,1)S(1)}, u32[]{:S(2)}, u32[]{:S(2)}) collective-permute-start(bf16[2,256,1024]{2,1,0:T(8,128)(2,1)S(1)} %copy-done.1), channel_id=1, source_target_pairs={{0,32},{16,48},{32,64},{48,80},{64,96},{80,112},{96,0},{112,16},{1... | collective-permute-start | bytes 3145736 | tf_op jit(solution)/shard_map/ppermute | solution.py:469
  57.8 96.3 %collective-permute-start.6 = (bf16[2,256,1024]{2,1,0:T(8,128)(2,1)S(1)}, bf16[2,256,1024]{2,1,0:T(8,128)(2,1)S(1)}, u32[]{:S(2)}, u32[]{:S(2)}) collective-permute-start(bf16[2,256,1024]{2,1,0:T(8,128)(2,1)S(1)} %copy-done.1), channel_id=1, source_target_pairs={{0,64},{16,80},{32,96},{48,112},{64,0},{80,16},{96,32},{112,48},{1... | collective-permute-start | bytes 3145736 | tf_op jit(solution)/shard_map/ppermute | solution.py:469
  60.7 93.4 %collective-permute-start.5 = (bf16[2,256,1024]{2,1,0:T(8,128)(2,1)S(1)}, bf16[2,256,1024]{2,1,0:T(8,128)(2,1)}, u32[]{:S(2)}, u32[]{:S(2)}) collective-permute-start(bf16[2,256,1024]{2,1,0:T(8,128)(2,1)S(1)} %copy-done.1), channel_id=1, source_target_pairs={{0,96},{16,112},{32,0},{48,16},{64,32},{80,48},{96,64},{112,80},{1... | collective-permute-start | bytes 3145736 | tf_op jit(solution)/shard_map/ppermute | solution.py:469
  154.1 1.0 copy-start.5
  154.1 1.3 copy-start.6
  173.6 28.1 %collective-permute-start.9 = (bf16[4,256,2048]{2,1,0:T(8,128)(2,1)}, bf16[4,256,2048]{2,1,0:T(8,128)(2,1)}, u32[]{:S(2)}, u32[]{:S(2)}) collective-permute-start(bf16[4,256,2048]{2,1,0:T(8,128)(2,1)} %get-tuple-element.32.mine), channel_id=1, source_target_pairs={{0,16},{16,0},{32,48},{48,32},{64,80},{80,64},{96,112},{112,96},{1... | collective-permute-start | bytes 12582920 | tf_op jit(solution)/shard_map/ppermute | solution.py:482
Sparse Core Ops, SparseCore 0:
  10.1 48.4 all-gather.3
  60.7 111.3 all-gather.5
